TPU v7x, 32 devices: a whole 2x2x4 slice. The times are simulated.
32 devices in a mesh: row: 2 (over y), col: 4 (over z), mp: 4 (over x, core).
Axes of the slice: x: 2, y: 2, z: 4, core: 2. Of those that a mesh axis runs over, the one named last changes fastest.
Arguments:
- hidden: bfloat16 [8192, 3584], P(('row', 'col'), 'mp'), may hold values from -6 to 6
- old_logp: float32 [8192], P(('row', 'col')), may hold values from -0.6 to 0.6
- rewards: float32 [64], P(('row', 'col')), may hold values from -4 to 4
- resp_dest: int32 [64], P(('row', 'col')), may hold values from 0 to 7, as said below
- resp_len: int32 [64], P(('row', 'col')), may hold values from 1 to 128, as said below
- resp_offset: int32 [64], P(('row', 'col')), may hold values from 0 to 511, as said below
- prompt_group: int32 [64], P(('row', 'col')), may hold values from 0 to 7, as said below
- attn_gain: bfloat16 [3584], replicated, may hold values from 0.099609375 to 1.8984375
- w_query: bfloat16 [3584, 3584], P(None, 'mp'), may hold values from -0.09375 to 0.09375
- q_bias: bfloat16 [3584], P('mp'), may hold values from -3 to 3
- w_key: bfloat16 [3584, 512], P(None, 'mp'), may hold values from -0.09375 to 0.09375
- k_bias: bfloat16 [512], P('mp'), may hold values from -6 to 6
- w_value: bfloat16 [3584, 512], P(None, 'mp'), may hold values from -0.09375 to 0.09375
- v_bias: bfloat16 [512], P('mp'), may hold values from -3 to 3
- w_out: bfloat16 [3584, 3584], P('mp'), may hold values from -0.5 to 0.5
- final_gain: bfloat16 [3584], replicated, may hold values from 0.099609375 to 1.8984375
- chosen_rows: bfloat16 [4096, 3584], P(('row', 'col', 'mp')), may hold values from -0.01171875 to 0.01171875
- log_normalizer: float32 [4096], P(('row', 'col', 'mp')), may hold values from -0.6 to 0.6
Outputs:
- objective: float32 [4096], P(('row', 'col', 'mp'))
- loss: float32 [], replicated
Inputs may be any that keep to these rules, and one draw needn't show every extreme that they name: `resp_dest`: ranks are numbered row index * 4 + col index. A rank's responses go to ranks of the same col index: exactly 4 of them to each such rank, itself included; so every rank receives exactly 8 responses. `resp_len`: the responses bound for one rank hold at most 512 tokens together; in every draw some rank's responses fill all 512 positions, and some response has exactly 128. `resp_offset`: responses bound for one rank lie end to end from position 0, without gaps or intersection. `prompt_group`: each of the 8 groups has exactly 8 responses.
All inputs are finite; a program needn't handle non-finite values.
Results may differ from a plain program's by a relative error of at most 0.0019.
Values may be sent and summed in bfloat16 or wider, within the bound.
A program may use at most 128 MiB of HBM per device.

v0:
```python
import jax
import jax.numpy as jnp
from jax import lax
from jax.sharding import PartitionSpec as P

HEAD = 128
GROUP_SIZE = 8


norm_eps = 1e-06
rope_theta = 1000000.0
clip_low = 0.2
clip_high = 0.28
std_floor = 1.0
mask_fill = -1e30


def rotary(matrix, positions):
    half_size = matrix.shape[-1] // 2
    exponents = jnp.arange(half_size, dtype=jnp.float32) * (2.0 / matrix.shape[-1])
    frequency = rope_theta ** (-exponents)
    angles = positions[:, None] * frequency[None, :]
    cosine_table = jnp.cos(angles)[:, None, :]
    sine_table = jnp.sin(angles)[:, None, :]
    first_half = matrix[..., :half_size]
    second_half = matrix[..., half_size:]
    return jnp.concatenate(
        [
            first_half * cosine_table - second_half * sine_table,
            second_half * cosine_table + first_half * sine_table,
        ],
        -1,
    )


def body(
    hidden,
    old_logp,
    rewards,
    resp_dest,
    resp_len,
    resp_offset,
    prompt_group,
    attn_gain,
    w_query,
    q_bias,
    w_key,
    k_bias,
    w_value,
    v_bias,
    w_out,
    final_gain,
    chosen_rows,
    log_normalizer,
):
    highest = lax.Precision.HIGHEST
    row_ranks = lax.axis_size("row")
    col_ranks = lax.axis_size("col")
    rank_count = row_ranks * col_ranks
    response_count = resp_dest.shape[0]
    per_peer = response_count // row_ranks
    group_count = rank_count * response_count // GROUP_SIZE
    slot_length = hidden.shape[0] // response_count
    feature_count = hidden.shape[1]
    pack_length = response_count * slot_length // 2
    shard_count = lax.axis_size("mp")
    row_count = pack_length // shard_count
    slot_iota = jnp.arange(response_count, dtype=jnp.int32)
    group_iota = jnp.arange(group_count, dtype=jnp.int32)
    dest_row = resp_dest // col_ranks
    earlier = (slot_iota[None, :] < slot_iota[:, None]) & (dest_row[None, :] == dest_row[:, None])
    slot_in_peer = jnp.sum(earlier.astype(jnp.int32), 1)
    send_slot = dest_row * per_peer + slot_in_peer
    selector = send_slot[None, :] == slot_iota[:, None]
    selector_wide = selector.astype(jnp.float32)
    send_rows = jnp.dot(
        selector.astype(jnp.bfloat16),
        hidden.reshape(response_count, slot_length * feature_count),
        preferred_element_type=jnp.float32,
    ).astype(jnp.bfloat16)
    send_rows = send_rows.reshape(row_ranks, per_peer * slot_length, feature_count)
    send_logp = jnp.dot(
        selector_wide, old_logp.reshape(response_count, slot_length), precision=highest
    )
    send_logp = send_logp.reshape(row_ranks, per_peer * slot_length)
    send_length = jnp.dot(selector_wide, resp_len.astype(jnp.float32), precision=highest)
    send_offset = jnp.dot(selector_wide, resp_offset.astype(jnp.float32), precision=highest)
    member = (prompt_group[:, None] == group_iota[None, :]).astype(jnp.float32)
    totals, squares = lax.psum(
        (
            jnp.dot(rewards, member, precision=highest),
            jnp.dot(rewards * rewards, member, precision=highest),
        ),
        ("row", "col"),
    )
    means = totals / GROUP_SIZE
    variance = jnp.maximum(squares / GROUP_SIZE - means * means, 0.0)
    means, scales = (means, jnp.maximum(jnp.sqrt(variance), std_floor))
    member_adv = (rewards - jnp.dot(member, means, precision=highest)) / jnp.dot(
        member, scales, precision=highest
    )
    send_info = jnp.stack(
        [send_length, send_offset, jnp.dot(selector_wide, member_adv, precision=highest)], 1
    )
    send_info = send_info.reshape(row_ranks, per_peer, send_info.shape[1])
    recv_rows = lax.all_to_all(send_rows, "row", split_axis=0, concat_axis=0, tiled=True)
    recv_logp, recv_info = (
        lax.all_to_all(send_logp, "row", split_axis=0, concat_axis=0, tiled=True),
        lax.all_to_all(send_info, "row", split_axis=0, concat_axis=0, tiled=True),
    )
    recv_info = recv_info.reshape(response_count, recv_info.shape[2])
    lengths = recv_info[:, 0].astype(jnp.int32)
    offsets = recv_info[:, 1].astype(jnp.int32)
    slots = jnp.arange(pack_length, dtype=jnp.int32)[:, None]
    covered = (slots >= offsets[None, :]) & (slots < (offsets + lengths)[None, :])
    occupied = jnp.any(covered, 1)
    within_all = slots - offsets[None, :]
    token_index = jnp.sum(jnp.where(covered, slot_iota[None, :] * slot_length + within_all, 0), 1)
    positions = jnp.sum(jnp.where(covered, within_all, 0), 1).astype(jnp.float32)
    segment = jnp.where(occupied, jnp.sum(jnp.where(covered, slot_iota[None, :], 0), 1), -1)
    flat_rows = recv_rows.reshape(-1, feature_count)
    all_rows = lax.all_gather(flat_rows, "mp", axis=1, tiled=True)
    gathered = jnp.where(occupied[:, None], all_rows[token_index], jnp.zeros((), jnp.bfloat16))
    inverse = lax.rsqrt(
        jnp.mean(jnp.square(gathered.astype(jnp.float32)), -1, keepdims=True) + norm_eps
    )
    normed = (gathered.astype(jnp.float32) * inverse * attn_gain.astype(jnp.float32)).astype(
        jnp.bfloat16
    )
    heads_local = w_query.shape[1] // HEAD
    key_heads = w_key.shape[1] // HEAD
    queries = jnp.dot(normed, w_query, preferred_element_type=jnp.float32) + q_bias.astype(
        jnp.float32
    )
    queries = rotary(queries.reshape(pack_length, heads_local, HEAD), positions).astype(
        jnp.bfloat16
    )
    key_rows = jnp.dot(normed, w_key, preferred_element_type=jnp.float32) + k_bias.astype(
        jnp.float32
    )
    key_rows = rotary(key_rows.reshape(pack_length, key_heads, HEAD), positions).astype(
        jnp.bfloat16
    )
    value_rows = (
        (jnp.dot(normed, w_value, preferred_element_type=jnp.float32) + v_bias.astype(jnp.float32))
        .astype(jnp.bfloat16)
        .reshape(pack_length, key_heads, HEAD)
    )
    grouped = queries.reshape(pack_length, key_heads, heads_local // key_heads, HEAD)
    block_size = min(512, pack_length)
    scores = jnp.einsum(
        "qkgd,ekd->kgqe", grouped, key_rows, preferred_element_type=jnp.float32
    ) * HEAD ** (-0.5)
    allowed = (segment[0:block_size, None] == segment[None, :block_size]) & (
        jnp.arange(block_size)[None, :] <= jnp.arange(0, block_size)[:, None]
    )
    scores = jnp.where(allowed, scores, mask_fill)
    highest_score = jnp.max(scores, -1, keepdims=True)
    exponent = jnp.exp(scores - highest_score)
    weights = (exponent / jnp.sum(exponent, -1, keepdims=True)).astype(jnp.bfloat16)
    block_out = jnp.einsum(
        "kgqe,ekd->qkgd", weights, value_rows, preferred_element_type=jnp.float32
    )
    pieces = block_out.reshape(block_size, heads_local * HEAD).astype(jnp.bfloat16)
    branch = lax.psum_scatter(
        jnp.dot(pieces, w_out, preferred_element_type=jnp.float32).astype(jnp.bfloat16),
        "mp",
        scatter_dimension=0,
        tiled=True,
    ).astype(jnp.float32)
    own_start = lax.axis_index("mp") * row_count
    residual = lax.dynamic_slice_in_dim(gathered, own_start, row_count, 0)
    residual_out = (residual.astype(jnp.float32) + branch).astype(jnp.bfloat16)
    final_rows = residual_out.astype(jnp.float32)
    final_inverse = lax.rsqrt(jnp.mean(final_rows * final_rows, -1, keepdims=True) + norm_eps)
    logits = jnp.sum(
        final_rows
        * final_inverse
        * final_gain.astype(jnp.float32)
        * chosen_rows.astype(jnp.float32),
        -1,
    )
    own_covered = lax.dynamic_slice_in_dim(covered, own_start, row_count, 0)
    own_occupied = lax.dynamic_slice_in_dim(occupied, own_start, row_count, 0)
    own_token = lax.dynamic_slice_in_dim(token_index, own_start, row_count, 0)
    own_old = jnp.where(own_occupied, recv_logp.reshape(-1)[own_token], 0.0)
    pair_adv = recv_info[:, 2]
    token_adv = jnp.sum(jnp.where(own_covered, pair_adv[None, :], 0.0), 1)
    ratios = jnp.exp(logits - log_normalizer - own_old)
    bounded = jnp.clip(ratios, 1.0 - clip_low, 1.0 + clip_high)
    objective = jnp.where(own_occupied, jnp.minimum(ratios * token_adv, bounded * token_adv), 0.0)
    loss_sum, counted = lax.psum(
        (jnp.sum(objective), jnp.sum(own_occupied.astype(jnp.float32))), ("row", "col", "mp")
    )
    return (objective, -loss_sum / counted)


def solution(mesh):
    return jax.shard_map(
        body,
        mesh=mesh,
        in_specs=(
            P(("row", "col"), "mp"),
            P(("row", "col")),
            P(("row", "col")),
            P(("row", "col")),
            P(("row", "col")),
            P(("row", "col")),
            P(("row", "col")),
            P(),
            P(None, "mp"),
            P("mp"),
            P(None, "mp"),
            P("mp"),
            P(None, "mp"),
            P("mp"),
            P("mp", None),
            P(),
            P(("row", "col", "mp"), None),
            P(("row", "col", "mp")),
        ),
        out_specs=(P(("row", "col", "mp")), P()),
        check_vma=False,
    )
```

profile of v0, /device:TPU:0, one launch (start us, length us, event | category | flops | bytes accessed | tf_op | source)
XLA Modules:
  0.0 247.5 jit_solution(9806434673147270967)
XLA Ops:
  8.8 2.3 reshape.259
  11.2 1.9 convolution_convert_fusion
  13.0 2.3 reshape.260
  15.5 27.1 %all_to_all.19 = bf16[2,512,896]{2,1,0:T(8,128)(2,1)} all-to-all(bf16[2,512,896]{2,1,0:T(8,128)(2,1)S(1)} %reshape.260), channel_id=1, replica_groups=mesh['row'=2,'col'=4,'mp'=4] {'row'}, dimensions={0} | all-to-all | bytes 3670016 | tf_op jit(solution)/shard_map/all_to_all | solution.py:106
  43.0 20.7 %all-reduce.1 = (f32[8]{0:T(128)S(1)}, f32[8]{0:T(128)S(1)}) all-reduce(f32[8]{0:T(128)S(1)} %convolution_bitcast_fusion.2, f32[8]{0:T(128)S(1)} %convolution_bitcast_fusion.4), channel_id=1, replica_groups=mesh['row'=2,'col'=4,'mp'=4] {'row','col'}, use_global_device_ids=true, to_apply=%region_2.3 | all-reduce | flops 16 | bytes 128 | tf_op jit(solution)/shard_map/psum | solution.py:89
  65.3 3.2 %all-to-all-start = ((f32[2,4,3]{1,2,0:T(4,128)}), f32[2,4,3]{1,2,0:T(4,128)S(1)}, u32[]{:S(2)}, u32[]{:S(2)}) async-start(f32[2,4,3]{1,2,0:T(4,128)} %copy.38), calls=%async_computation | async-start | bytes 8192 | tf_op jit(solution)/shard_map/all_to_all | solution.py:109
  69.2 3.1 %all-to-all-done = f32[2,4,3]{1,2,0:T(4,128)S(1)} async-done(((f32[2,4,3]{1,2,0:T(4,128)}), f32[2,4,3]{1,2,0:T(4,128)S(1)}, u32[]{:S(2)}, u32[]{:S(2)}) %all-to-all-start) | async-done | bytes 128 | tf_op jit(solution)/shard_map/all_to_all | solution.py:109
  74.5 1.0 multiply_cosine_fusion
  75.5 20.0 %all-gather.2.cloned.1.call-done = bf16[1024,3584]{1,0:T(8,128)(2,1)} async-done(((bf16[1024,896]{1,0:T(8,128)(2,1)}), bf16[1024,3584]{1,0:T(8,128)(2,1)}) %all-gather.2.cloned.1.call-update) | async-done | bytes 7340048 | tf_op jit(solution)/shard_map/all_gather | solution.py:122
  95.5 12.1 %gather_fusion = bf16[512,3584]{1,0:T(8,128)(2,1)} fusion(bf16[1024,3584]{1,0:T(8,128)(2,1)} %all-gather.2.cloned.1.call-done, s32[1024]{0:T(1024)S(1)} %pad_clamp_fusion.1), kind=kCustom, calls=%fused_computation | custom fusion | bytes 7342080 | tf_op jit(solution)/shard_map/gather | solution.py:123
  107.6 3.4 %fusion = (f32[512]{0:T(512)S(1)}, bf16[512,3584]{1,0:T(8,128)(2,1)S(1)}) fusion(bf16[512,3584]{1,0:T(8,128)(2,1)} %gather_fusion, pred[512]{0:T(512)(128)(4,1)S(1)} %get-tuple-element.23), kind=kLoop, calls=%fused_computation.5 | loop fusion | flops 7339520 | bytes 7342592 | tf_op jit(solution)/shard_map/reduce_sum | solution.py:125
  111.0 1.5 fusion.15
  112.5 1.2 fusion.38
  114.0 5.3 %convolution_add_fusion = f32[512,896]{1,0:T(8,128)} fusion(bf16[3584,896]{1,0:T(8,128)(2,1)S(1)} %bitcast.112, f32[896]{0:T(1024)S(1)} %convert_element_type.129, bf16[512,3584]{1,0:T(8,128)(2,1)S(1)} %get-tuple-element.12, f32[3584]{0:T(1024)S(1)} %convert_element_type.123, f32[512]{0:T(512)S(1)} %add_rsqrt_fusion), kind=kOutput, calls=%fused_computation.27 | convolution fusion | flops 3296133120 | bytes 11947520 | tf_op jit(solution)/shard_map/dot_general | solution.py:132
  119.3 2.0 copy.40
  121.3 1.5 fusion.78
  122.8 1.7 copy.52
  124.5 3.0 %copy.53 = f32[512,7,64]{2,0,1:T(8,128)} copy(f32[512,7,64]{0,2,1:T(8,128)} %get-tuple-element.15) | data formatting | bytes 1835008
  127.5 2.0 subtract_convert_fusion
  129.6 2.1 fusion.4
  131.6 2.9 %copy-done.1 = f32[512,512,7]{1,0,2:T(8,128)} copy-done((f32[512,512,7]{1,0,2:T(8,128)}, f32[512,512,7]{1,0,2:T(8,128)S(1)}, u32[]{:S(2)}) %copy-start.1) | copy-done | bytes 7340056
  134.6 1.6 fusion.3
  136.2 7.6 %fusion.12 = bf16[128,7,512]{2,0,1:T(8,128)(2,1)S(1)} fusion(f32[7,512]{1,0:T(8,128)S(1)} %fusion.3, f32[7,512]{1,0:T(8,128)S(1)} %get-tuple-element.26, f32[512,512,7]{1,0,2:T(8,128)} %copy-done.1, pred[512,512]{0,1:T(8,128)(4,1)S(1)} %fusion.21, bf16[3584,128]{1,0:T(8,128)(2,1)S(1)} %copy-done, f32[128]{0:T(128)S(1)} %copy-done.26, ...), kind=kOutput, calls=%fused_computation.28 | convolution fusion | flops 956628992 | bytes 13152768 | tf_op jit(solution)/shard_map/kgqe,ekd->qkgd/dot_general | solution.py:161
  143.8 8.3 %convolution_convert_fusion.1 = bf16[512,3584]{1,0:T(8,128)(2,1)} fusion(bf16[512,896]{0,1:T(8,128)(2,1)S(1)} %bitcast.113, bf16[896,3584]{1,0:T(8,128)(2,1)} %param.32), kind=kOutput, calls=%fused_computation.12 | convolution fusion | flops 3290169344 | bytes 11010048 | tf_op jit(solution)/shard_map/dot_general | solution.py:166
  153.5 3.2 %all-to-all-start.2 = ((f32[2,1,512]{2,1,0:T(1,128)}), f32[2,1,512]{2,1,0:T(1,128)S(1)}, u32[]{:S(2)}, u32[]{:S(2)}) async-start(f32[2,1,512]{2,1,0:T(1,128)} %bitcast.32), calls=%async_computation.3 | async-start | bytes 8192 | tf_op jit(solution)/shard_map/all_to_all | solution.py:108
  158.2 2.2 all-to-all-done.2
  160.5 1.0 gather_fusion.1
  161.4 32.1 %reduce-scatter.2.cloned.1.call-done = bf16[128,3584]{1,0:T(8,128)(2,1)} async-done(((bf16[512,3584]{1,0:T(8,128)(2,1)}), bf16[128,3584]{1,0:T(8,128)(2,1)}) %reduce-scatter.2.cloned.1.call-update) | async-done | bytes 917520 | tf_op jit(solution)/shard_map/reduce_scatter | solution.py:165
  193.5 1.8 fusion.8
  195.4 2.1 fusion.11
  197.5 1.3 fusion.77
  198.7 39.6 %all-reduce = (f32[]{:T(128)}, f32[]{:T(128)}) all-reduce(f32[]{:T(128)} %get-tuple-element.9, f32[]{:T(128)} %get-tuple-element.25), channel_id=1, replica_groups=mesh['row'=2,'col'=4,'mp'=4] {'row','col','mp'}, use_global_device_ids=true, to_apply=%region_15.16 | all-reduce | flops 2 | bytes 16 | tf_op jit(solution)/shard_map/psum | solution.py:192
  (100 shorter events, 9.7 us)
Async XLA Ops:
  7.2 129.0 %copy-start = (bf16[3584,128]{1,0:T(8,128)(2,1)S(1)}, bf16[3584,128]{1,0:T(8,128)(2,1)}, u32[]{:S(2)}) copy-start(bf16[3584,128]{1,0:T(8,128)(2,1)} %param.30) | copy-start | bytes 2752516
  7.2 88.3 %all-gather.2.cloned.1.call-start = ((), (), s32[]{:S(2)}) async-start(), calls=%async_computation.4 | async-start | bytes 9175040 | tf_op jit(solution)/shard_map/all_gather | solution.py:122
  8.8 55.7 %copy-start.16 = (s32[8]{0:T(128)}, s32[8]{0:T(128)S(1)}, u32[]{:S(2)}) copy-start(s32[8]{0:T(128)S(1)} %multiply_add_fusion) | copy-start | bytes 100
  15.4 27.2 %copy-start.20 = (s32[8]{0:T(128)S(1)}, s32[8]{0:T(128)}, u32[]{:S(2)}) copy-start(s32[8]{0:T(128)} %param.24) | copy-start | bytes 100
  15.4 27.2 %copy-start.21 = (f32[8]{0:T(128)S(1)}, f32[8]{0:T(128)}, u32[]{:S(2)}) copy-start(f32[8]{0:T(128)} %param.20) | copy-start | bytes 100
  15.4 48.9 %copy-start.22 = (s32[8]{0:T(128)S(1)}, s32[8]{0:T(128)}, u32[]{:S(2)}) copy-start(s32[8]{0:T(128)} %param.22) | copy-start | bytes 100
  15.4 49.1 %copy-start.23 = (s32[8]{0:T(128)S(1)}, s32[8]{0:T(128)}, u32[]{:S(2)}) copy-start(s32[8]{0:T(128)} %param.23) | copy-start | bytes 100
  15.4 53.2 %copy-start.8 = (bf16[3584]{0:T(1024)(128)(2,1)S(1)}, bf16[3584]{0:T(1024)(128)(2,1)}, u32[]{:S(2)}) copy-start(bf16[3584]{0:T(1024)(128)(2,1)} %param.25) | copy-start | bytes 21508
  15.4 53.2 %copy-start.24 = (bf16[128]{0:T(256)(128)(2,1)S(1)}, bf16[128]{0:T(256)(128)(2,1)}, u32[]{:S(2)}) copy-start(bf16[128]{0:T(256)(128)(2,1)} %param.29) | copy-start | bytes 772
  15.4 53.2 %copy-start.12 = (bf16[896]{0:T(1024)(128)(2,1)S(1)}, bf16[896]{0:T(1024)(128)(2,1)}, u32[]{:S(2)}) copy-start(bf16[896]{0:T(1024)(128)(2,1)} %param.27) | copy-start | bytes 5380
  15.4 53.2 %copy-start.25 = (bf16[128]{0:T(256)(128)(2,1)S(1)}, bf16[128]{0:T(256)(128)(2,1)}, u32[]{:S(2)}) copy-start(bf16[128]{0:T(256)(128)(2,1)} %param.31) | copy-start | bytes 772
  65.3 7.0 %all-to-all-start = ((f32[2,4,3]{1,2,0:T(4,128)}), f32[2,4,3]{1,2,0:T(4,128)S(1)}, u32[]{:S(2)}, u32[]{:S(2)}) async-start(f32[2,4,3]{1,2,0:T(4,128)} %copy.38), calls=%async_computation | async-start | bytes 8192 | tf_op jit(solution)/shard_map/all_to_all | solution.py:109
  68.5 125.0 %reduce-scatter.2.cloned.1.call-start = ((), (), s32[]{:S(2)}) async-start(), calls=%async_computation.5 | async-start | bytes 4587520 | tf_op jit(solution)/shard_map/reduce_scatter | solution.py:165
  74.3 33.3 %copy-start.6 = (pred[512]{0:T(512)(128)(4,1)}, pred[512]{0:T(512)(128)(4,1)S(1)}, u32[]{:S(2)}) copy-start(pred[512]{0:T(512)(128)(4,1)S(1)} %get-tuple-element.23) | copy-start | bytes 1540
  107.6 3.4 %copy-start.19 = (bf16[3584,128]{1,0:T(8,128)(2,1)S(1)}, bf16[3584,128]{1,0:T(8,128)(2,1)}, u32[]{:S(2)}) copy-start(bf16[3584,128]{1,0:T(8,128)(2,1)} %param.28) | copy-start | bytes 2752516
  107.6 6.2 %slice-start = ((s8[6422528]{0:T(1024)(128)(4,1)}), s8[4194304]{0:T(1024)(128)(4,1)S(1)}, s32[]{:S(2)}) async-start(s8[6422528]{0:T(1024)(128)(4,1)} %bitcast.111), calls=%async_computation.6 | async-start | bytes 8388608
  111.0 2.8 %copy-start.2 = (bf16[512,3584]{1,0:T(8,128)(2,1)}, bf16[512,3584]{1,0:T(8,128)(2,1)S(1)}, u32[]{:S(2)}) copy-start(bf16[512,3584]{1,0:T(8,128)(2,1)S(1)} %get-tuple-element.12) | copy-start | bytes 11010052
  111.0 2.7 %copy-start.13 = (f32[512]{0:T(512)}, f32[512]{0:T(512)S(1)}, u32[]{:S(2)}) copy-start(f32[512]{0:T(512)S(1)} %add_rsqrt_fusion) | copy-start | bytes 6148
  111.0 3.0 %slice-start.1 = ((s8[6422528]{0:T(1024)(128)(4,1)}), s8[2228224]{0:T(1024)(128)(4,1)S(1)}, s32[]{:S(2)}) async-start(s8[6422528]{0:T(1024)(128)(4,1)} %bitcast.111), calls=%async_computation.7 | async-start | bytes 4456448
  127.5 2.0 copy-start.4
  127.5 2.0 copy-start.5
  131.6 3.0 %copy-start.1 = (f32[512,512,7]{1,0,2:T(8,128)}, f32[512,512,7]{1,0,2:T(8,128)S(1)}, u32[]{:S(2)}) copy-start(f32[512,512,7]{1,0,2:T(8,128)S(1)} %get-tuple-element.27) | copy-start | bytes 22020100
  134.6 1.6 copy-start.14
  134.6 1.6 copy-start.26
  152.0 0.7 copy-start.11
  152.0 0.7 copy-start.17
  152.0 4.6 %copy-start.9 = (bf16[3584]{0:T(1024)(128)(2,1)S(1)}, bf16[3584]{0:T(1024)(128)(2,1)}, u32[]{:S(2)}) copy-start(bf16[3584]{0:T(1024)(128)(2,1)} %param.33) | copy-start | bytes 21508
  152.1 5.4 %copy-start.15 = (f32[8]{0:T(128)S(1)}, f32[8]{0:T(128)}, u32[]{:S(2)}) copy-start(f32[8]{0:T(128)} %get-tuple-element.21) | copy-start | bytes 100
  152.1 43.3 %copy-start.3 = (bf16[128,3584]{1,0:T(8,128)(2,1)S(1)}, bf16[128,3584]{1,0:T(8,128)(2,1)}, u32[]{:S(2)}) copy-start(bf16[128,3584]{1,0:T(8,128)(2,1)} %param.34) | copy-start | bytes 2752516
  152.1 45.4 %copy-start.7 = (pred[512]{0:T(512)(128)(4,1)S(1)}, pred[512]{0:T(512)(128)(4,1)}, u32[]{:S(2)}) copy-start(pred[512]{0:T(512)(128)(4,1)} %copy-done.6) | copy-start | bytes 1540
  152.1 45.4 %copy-start.18 = (f32[128]{0:T(128)S(1)}, f32[128]{0:T(128)}, u32[]{:S(2)}) copy-start(f32[128]{0:T(128)} %param.35) | copy-start | bytes 1540
  153.5 7.0 %all-to-all-start.2 = ((f32[2,1,512]{2,1,0:T(1,128)}), f32[2,1,512]{2,1,0:T(1,128)S(1)}, u32[]{:S(2)}, u32[]{:S(2)}) async-start(f32[2,1,512]{2,1,0:T(1,128)} %bitcast.32), calls=%async_computation.3 | async-start | bytes 8192 | tf_op jit(solution)/shard_map/all_to_all | solution.py:108
  (1 other events, 0.6 us)
Sparse Core Ops, SparseCore 0:
  42.7 52.6 all-gather.1
  152.2 41.2 reduce-scatter.1
where the time goes:
time: 248 us
  blocking collectives  87.4 us (35%)
  waiting for transfers between devices  57.4 us (23%)
  local copies, waits for them, and re-layouts  31.4 us (13%)
  matrix products  28.4 us (11%)
  other arithmetic  19.6 us (8%)
  between operations  16.9 us (7%)
  starting transfers between devices  6.51 us (3%)
    psum x1, blocking collectives, body(): lax.psum((jnp.sum(objective), jnp.sum(own_occupied.astype(jnp.float32))),...  39.6 us
    reduce_scatter x1, waiting for transfers between devices, body(): lax.psum_scatter(jnp.dot(pieces, w_out, preferred_element_type=jnp.float3...  32.1 us
    all_to_all x1, blocking collectives, body(): lax.all_to_all(send_rows, 'row', split_axis=0, concat_axis=0, tiled=True)  27.1 us
    psum x1, blocking collectives, body(): lax.psum((jnp.dot(rewards, member, precision=highest), jnp.dot(rewards *...  20.7 us
    all_gather x1, waiting for transfers between devices, body(): all_rows = lax.all_gather(flat_rows, 'mp', axis=1, tiled=True)  20 us
    gather x1, local copies, waits for them, and re-layouts, body(): all_rows[token_index]  12.1 us
    unnamed x60, local copies, waits for them, and re-layouts  9.17 us
    dot_general x1, matrix products, body(): jnp.dot(pieces, w_out, preferred_element_type=jnp.float32)  8.28 us
  transfers between devices with their start and end apart: 4, of which 4 were waited for; matrix products, arithmetic and copies ran while one was open for 3% of the time, Pallas kernels for 0%

commit v1 on v0

v1 whole, which is shorter than its diff:
```python
import functools

import jax
import jax.numpy as jnp
import numpy as np
from jax import lax
from jax.experimental import pallas as pl
from jax.experimental.pallas import tpu as pltpu
from jax.sharding import PartitionSpec as P

HEAD = 128
GROUP_SIZE = 8
MESH = pl.DeviceIdType.MESH

norm_eps = 1e-06
rope_theta = 1000000.0
clip_low = 0.2
clip_high = 0.28
std_floor = 1.0
mask_fill = -1e30
VMEM = pl.BlockSpec(memory_space=pltpu.VMEM)
ANY = pl.BlockSpec(memory_space=pl.ANY)


def rank_peers(rows, cols):
    r, c = lax.axis_index("row"), lax.axis_index("col")
    return [
        {"row": lax.rem(r + i, rows), "col": lax.rem(c + j, cols)}
        for i in range(rows)
        for j in range(cols)
        if i or j
    ]


def main_kernel(
    rows,
    cols,
    hidden_hbm,
    logp,
    reward_in,
    dest_in,
    len_in,
    off_in,
    group_in,
    gain,
    wq_hbm,
    qb,
    wk_hbm,
    kb,
    wv_hbm,
    vb,
    wo_hbm,
    freq,
    normalizer,
    chosen_hbm,
    fgain,
    obj_ref,
    loss_ref,
    hidden,
    meta,
    everything,
    outgoing,
    recv,
    x,
    wq,
    wk,
    wv,
    wo,
    chosen,
    kbuf,
    vbuf,
    seg,
    pos,
    mixed,
    ptmp,
    r_comb,
    r_pair,
    r_cross,
    lsend,
    lrecv,
    lsend2,
    lrecv2,
    w_sem,
    f_send,
    f_recv,
    ex_send,
    ex_recv,
    g_send,
    g_recv,
    rs_send,
    rs_recv,
    l_send,
    l_recv,
    l2_send,
    l2_recv,
):
    me = lax.axis_index("mp")
    row = lax.axis_index("row")
    pair = me + 1 - 2 * lax.rem(me, 2)
    cross = lax.rem(me + 2, 4)
    diag = lax.rem(pair + 2, 4)
    mp_peers = (pair, cross, diag)
    peers = rank_peers(rows, cols)
    pack, width = x.shape
    feats = hidden.shape[1]
    count, slot = logp.shape
    blocks = width // feats
    chunk = pack // blocks
    heads = wq.shape[1] // HEAD

    load = pltpu.make_async_copy(hidden_hbm, hidden, w_sem.at[5])
    load.start()
    weights = [
        pltpu.make_async_copy(src, dst, w_sem.at[i])
        for i, (src, dst) in enumerate(
            ((wq_hbm, wq), (wk_hbm, wk), (wv_hbm, wv), (wo_hbm, wo), (chosen_hbm, chosen))
        )
    ]
    for copy in weights:
        copy.start()

    def iota(shape, dim):
        return lax.broadcasted_iota(jnp.int32, shape, dim)

    def upright(line):
        n = line.shape[1]
        return jnp.sum(jnp.where(iota((n, n), 0) == iota((n, n), 1), line, 0.0), 1, keepdims=True)

    def flat_of(column):
        n = column.shape[0]
        return jnp.sum(jnp.where(iota((n, n), 0) == iota((n, n), 1), column, 0.0), 0, keepdims=True)

    facts = [
        upright(ref[...].astype(jnp.float32))
        for ref in (reward_in, dest_in, len_in, off_in, group_in)
    ]
    tile = jnp.zeros((count, 128), jnp.float32)
    for i, fact in enumerate(facts):
        tile = jnp.where(iota(tile.shape, 1) == i, fact, tile)
    meta[:, 0:slot] = logp[...]
    meta[:, slot : slot + 128] = tile

    barrier = pltpu.get_barrier_semaphore()
    for peer in peers:
        pl.semaphore_signal(barrier, inc=1, device_id=peer, device_id_type=MESH)
    for peer in mp_peers:
        pl.semaphore_signal(barrier, inc=1, device_id={"mp": peer}, device_id_type=MESH)
    pl.semaphore_wait(barrier, len(peers) + len(mp_peers))

    def span(c):
        return pl.ds(pl.multiple_of(c * chunk, chunk), chunk)

    def lanes(d):
        return pl.ds(pl.multiple_of(d * feats, 128), feats)

    def exchange(k, c):
        return pltpu.make_async_remote_copy(
            src_ref=outgoing.at[k - 1, span(c)],
            dst_ref=recv.at[k - 1, span(c)],
            send_sem=ex_send.at[k - 1, c],
            recv_sem=ex_recv.at[k - 1, c],
            device_id={"row": lax.rem(row + k, rows)},
            device_id_type=MESH,
        )

    shared = []
    for k, peer in enumerate(peers):
        copy = pltpu.make_async_remote_copy(
            src_ref=meta,
            dst_ref=everything.at[k + 1],
            send_sem=f_send.at[k],
            recv_sem=f_recv.at[k],
            device_id=peer,
            device_id_type=MESH,
        )
        copy.start()
        shared.append(copy)
    everything[0] = meta[...]
    load.wait()
    column = lax.axis_index("col")
    _, dest, length, offset, _ = facts

    def packed(k, c):
        to = (lax.rem(row + k, rows) * cols + column).astype(jnp.float32)
        within = (c * chunk + iota((count, chunk), 1)).astype(jnp.float32) - offset
        hit = (dest == to) & (within >= 0.0) & (within < length)
        base = (iota((count, chunk), 0) * slot + 1).astype(jnp.float32)
        source = jnp.sum(jnp.where(hit, base + within, 0.0), 0, keepdims=True) - 1.0
        source = upright(source).astype(jnp.int32)
        chooser = jnp.where(iota((chunk, count * slot), 1) == source, 1.0, 0.0)
        return jnp.dot(
            chooser.astype(jnp.bfloat16), hidden[...], preferred_element_type=jnp.float32
        ).astype(jnp.bfloat16)

    def pack_out(c, carry):
        for k in range(1, rows):
            outgoing[k - 1, span(c), :] = packed(k, c)

            @pl.when(c == 0)
            def _():
                exchange(k, c).start()

        return carry

    def pack_own(c, carry):
        x[span(c), lanes(me)] = packed(0, c)
        return carry

    lax.fori_loop(0, blocks, pack_out, 0)
    lax.fori_loop(0, blocks, pack_own, 0)

    for copy in shared:
        copy.wait_recv()
    total_count = rows * cols * count
    table = everything[...].reshape(total_count, slot + 128)
    reward, dest, length, offset, group = (table[:, slot + i : slot + i + 1] for i in range(5))
    same = jnp.where(group == flat_of(group), 1.0, 0.0)
    centered = reward - jnp.sum(same * flat_of(reward), 1, keepdims=True) / GROUP_SIZE
    spread = flat_of(centered)
    spread = jnp.sum(same * (spread * spread), 1, keepdims=True) / GROUP_SIZE
    advantage = centered / jnp.maximum(jnp.sqrt(spread), std_floor)
    rank = (row * cols + column).astype(jnp.float32)

    def cover(first, size):
        within = (first + iota((total_count, size), 1)).astype(jnp.float32) - offset
        return (dest == rank) & (within >= 0.0) & (within < length), within

    covered, within = cover(me * chunk, chunk)
    token = jnp.sum(jnp.where(covered, within, 0.0), 0, keepdims=True)
    mine = jnp.where(covered, 1.0, 0.0)
    adv = jnp.sum(jnp.where(covered, advantage, 0.0), 0, keepdims=True)
    occupied = jnp.sum(mine, 0, keepdims=True)
    olds = lax.dot_general(
        table[:, :slot],
        mine,
        (((0,), (0,)), ((), ())),
        precision=lax.Precision.HIGHEST,
        preferred_element_type=jnp.float32,
    )
    old = jnp.sum(
        jnp.where(iota(olds.shape, 0).astype(jnp.float32) == token, olds, 0.0), 0, keepdims=True
    )
    counted = jnp.sum(jnp.broadcast_to(length, (total_count, chunk)), 0, keepdims=True)
    covered, within = cover(0, pack)
    which = (iota((total_count, pack), 0) + 1).astype(jnp.float32)
    seg[:, chunk : chunk + pack] = jnp.sum(jnp.where(covered, which, 0.0), 0, keepdims=True)
    seg[:, 0:chunk] = jnp.full((1, chunk), -1.0, jnp.float32)
    pos[...] = jnp.sum(jnp.where(covered, within, 0.0), 0, keepdims=True)

    def gather(kind, c):
        owner = cross if kind == 2 else me
        place = x.at[span(c), lanes(owner)]
        return pltpu.make_async_remote_copy(
            src_ref=place,
            dst_ref=place,
            send_sem=g_send.at[kind, c],
            recv_sem=g_recv.at[kind, c],
            device_id={"mp": cross if kind == 1 else pair},
            device_id_type=MESH,
        )

    def gathered(kind, c):
        owner = (pair, cross, diag)[kind]
        place = x.at[span(c), lanes(owner)]
        return pltpu.make_async_remote_copy(
            src_ref=place,
            dst_ref=place,
            send_sem=g_send.at[kind, c],
            recv_sem=g_recv.at[kind, c],
            device_id={"mp": cross if kind == 1 else pair},
            device_id_type=MESH,
        )

    def stage_a(c):
        for k in range(1, rows):
            exchange(k, c).wait()

            @pl.when(c + 1 < blocks)
            def _():
                exchange(k, c + 1).start()

        total = x[span(c), lanes(me)]
        for k in range(1, rows):
            total = total + recv[k - 1, span(c), :]
        x[span(c), lanes(me)] = total
        gather(1, c).start()
        gather(0, c).start()

    def scatter(kind, c, s):
        target = (r_comb, r_pair, r_cross)[kind]
        return pltpu.make_async_remote_copy(
            src_ref=ptmp.at[c, :, pl.ds(s * feats, feats)],
            dst_ref=target.at[:, pl.ds(s * feats, feats)],
            send_sem=rs_send.at[kind, s],
            recv_sem=rs_recv.at[kind, s],
            device_id={"mp": cross if kind == 2 else pair},
            device_id_type=MESH,
        )

    kbuf[0:chunk, :] = jnp.zeros((chunk, HEAD), kbuf.dtype)
    vbuf[0:chunk, :] = jnp.zeros((chunk, HEAD), vbuf.dtype)
    stage_a(0)
    for copy in weights:
        copy.wait()

    def step(c, carry):
        @pl.when(c + 1 < blocks)
        def _():
            stage_a(c + 1)

        gathered(1, c).wait_recv()
        gather(2, c).start()
        gathered(0, c).wait_recv()
        gathered(2, c).wait_recv()
        wide = x[span(c), :].astype(jnp.float32)
        inverse = lax.rsqrt(jnp.mean(wide * wide, -1, keepdims=True) + norm_eps)
        normed = (wide * inverse * gain[...].astype(jnp.float32)).astype(jnp.bfloat16)
        angles = upright(pos[:, span(c)]) * freq[...]
        cos_c, sin_c = jnp.cos(angles), jnp.sin(angles)
        sin_c = jnp.where(iota(angles.shape, 1) < HEAD // 2, -sin_c, sin_c)

        def rope(value):
            return (value * cos_c + pltpu.roll(value, HEAD // 2, 1) * sin_c).astype(jnp.bfloat16)

        after = pl.ds(pl.multiple_of((c + 1) * chunk, chunk), chunk)
        window = pl.ds(pl.multiple_of(c * chunk, chunk), 2 * chunk)
        key = jnp.dot(normed, wk[...], preferred_element_type=jnp.float32)
        kbuf[after, :] = rope(key + kb[...].astype(jnp.float32))
        value = jnp.dot(normed, wv[...], preferred_element_type=jnp.float32)
        vbuf[after, :] = (value + vb[...].astype(jnp.float32)).astype(jnp.bfloat16)
        query = jnp.dot(normed, wq[...], preferred_element_type=jnp.float32)
        query = query + qb[...].astype(jnp.float32)
        keys, values = kbuf[window, :], vbuf[window, :]
        shape = (chunk, 2 * chunk)
        allowed = (upright(seg[:, after]) == seg[:, window]) & (
            lax.broadcasted_iota(jnp.int32, shape, 1)
            <= lax.broadcasted_iota(jnp.int32, shape, 0) + chunk
        )
        for h in range(heads):
            cut = slice(h * HEAD, (h + 1) * HEAD)
            scores = lax.dot_general(
                rope(query[:, cut]),
                keys,
                (((1,), (1,)), ((), ())),
                preferred_element_type=jnp.float32,
            ) * HEAD ** (-0.5)
            scores = jnp.where(allowed, scores, mask_fill)
            exponent = jnp.exp(scores - jnp.max(scores, -1, keepdims=True))
            share = (exponent / jnp.sum(exponent, -1, keepdims=True)).astype(jnp.bfloat16)
            mixed[:, cut] = jnp.dot(share, values, preferred_element_type=jnp.float32).astype(
                jnp.bfloat16
            )
        for s in range(blocks):
            cut = slice(s * feats, (s + 1) * feats)
            ptmp[c, :, cut] = jnp.dot(
                mixed[...], wo[:, cut], preferred_element_type=jnp.float32
            ).astype(jnp.bfloat16)

            @pl.when(c == diag)
            def _():
                scatter(0, c, s).start()

            @pl.when(c == pair)
            def _():
                scatter(1, c, s).start()

        @pl.when(c == cross)
        def _():
            for s in range(blocks):
                cut = slice(s * feats, (s + 1) * feats)
                scatter(0, c, s).wait_recv()
                ptmp[c, :, cut] = (
                    ptmp[c, :, cut].astype(jnp.float32) + r_comb[:, cut].astype(jnp.float32)
                ).astype(jnp.bfloat16)
                scatter(2, c, s).start()

        return carry

    lax.fori_loop(0, blocks, step, 0)

    squares = jnp.zeros((chunk, 1), jnp.float32)
    product = jnp.zeros((chunk, 1), jnp.float32)
    for s in range(blocks):
        cut = slice(s * feats, (s + 1) * feats)
        scatter(1, me, s).wait_recv()
        scatter(2, me, s).wait_recv()
        branch = (
            ptmp[me, :, cut].astype(jnp.float32)
            + r_pair[:, cut].astype(jnp.float32)
            + r_cross[:, cut].astype(jnp.float32)
        )
        final = (x[span(me), cut].astype(jnp.float32) + branch).astype(jnp.bfloat16)
        final = final.astype(jnp.float32)
        squares = squares + jnp.sum(final * final, -1, keepdims=True)
        product = product + jnp.sum(
            final * fgain[:, cut].astype(jnp.float32) * chosen[:, cut].astype(jnp.float32),
            -1,
            keepdims=True,
        )
    logits = product * lax.rsqrt(squares / width + norm_eps)
    eye = lax.broadcasted_iota(jnp.int32, (chunk, chunk), 0) == lax.broadcasted_iota(
        jnp.int32, (chunk, chunk), 1
    )
    logits = jnp.sum(jnp.where(eye, logits, 0.0), 0, keepdims=True)
    ratios = jnp.exp(logits - normalizer[...] - old)
    bounded = jnp.clip(ratios, 1.0 - clip_low, 1.0 + clip_high)
    objective = jnp.where(occupied > 0.5, jnp.minimum(ratios * adv, bounded * adv), 0.0)
    obj_ref[...] = objective

    total = jnp.broadcast_to(jnp.sum(objective, -1, keepdims=True), lsend.shape)
    lsend[...] = total
    lrecv[me] = total
    copies = []
    for k, peer in enumerate(mp_peers):
        copy = pltpu.make_async_remote_copy(
            src_ref=lsend,
            dst_ref=lrecv.at[me],
            send_sem=l_send.at[k],
            recv_sem=l_recv.at[k],
            device_id={"mp": peer},
            device_id_type=MESH,
        )
        copy.start()
        copies.append(copy)
    for copy in shared:
        copy.wait_send()
    for c in range(blocks):
        for kind in range(3):
            gather(kind, c).wait_send()
    for s in range(blocks):
        scatter(0, diag, s).wait_send()
        scatter(1, pair, s).wait_send()
        scatter(2, cross, s).wait_send()
    for copy in copies:
        copy.wait()
    rank = row * cols + column
    total = lrecv[0]
    for k in range(1, blocks):
        total = total + lrecv[k]
    lsend2[...] = total
    lrecv2[rank] = total
    copies = []
    for k, peer in enumerate(peers):
        copy = pltpu.make_async_remote_copy(
            src_ref=lsend2,
            dst_ref=lrecv2.at[rank],
            send_sem=l2_send.at[k],
            recv_sem=l2_recv.at[k],
            device_id=peer,
            device_id_type=MESH,
        )
        copy.start()
        copies.append(copy)
    for copy in copies:
        copy.wait()
    total = lrecv2[0]
    for k in range(1, rows * cols):
        total = total + lrecv2[k]
    loss_ref[...] = -total[0:1, :] / counted


def body(
    hidden,
    old_logp,
    rewards,
    resp_dest,
    resp_len,
    resp_offset,
    prompt_group,
    attn_gain,
    w_query,
    q_bias,
    w_key,
    k_bias,
    w_value,
    v_bias,
    w_out,
    final_gain,
    chosen_rows,
    log_normalizer,
):
    rows, cols, mp = lax.axis_size("row"), lax.axis_size("col"), lax.axis_size("mp")
    ranks = rows * cols
    count = resp_dest.shape[0]
    slot, feats = hidden.shape[0] // count, hidden.shape[1]
    own_rows, width = chosen_rows.shape
    pack = own_rows * mp
    half = np.arange(HEAD, dtype=np.float32) % (HEAD // 2)
    freq = np.float32(rope_theta) ** (-(half * np.float32(2.0 / HEAD)))
    freq = freq.astype(np.float32)[None, :]
    dma = pltpu.SemaphoreType.DMA
    bf16, f32 = jnp.bfloat16, jnp.float32
    objective, loss = pl.pallas_call(
        functools.partial(main_kernel, rows, cols),
        out_shape=(
            jax.ShapeDtypeStruct((1, own_rows), f32),
            jax.ShapeDtypeStruct((1, own_rows), f32),
        ),
        in_specs=[ANY]
        + [VMEM] * 7
        + [ANY, VMEM, ANY, VMEM, ANY, VMEM, ANY, VMEM, VMEM, ANY, VMEM],
        out_specs=(VMEM, VMEM),
        scratch_shapes=[
            pltpu.VMEM(hidden.shape, bf16),
            pltpu.VMEM((count, slot + 128), f32),
            pltpu.VMEM((ranks, count, slot + 128), f32),
            pltpu.VMEM((max(rows - 1, 1), pack, feats), bf16),
            pltpu.VMEM((max(rows - 1, 1), pack, feats), bf16),
            pltpu.VMEM((pack, width), bf16),
            pltpu.VMEM(w_query.shape, bf16),
            pltpu.VMEM(w_key.shape, bf16),
            pltpu.VMEM(w_value.shape, bf16),
            pltpu.VMEM(w_out.shape, bf16),
            pltpu.VMEM(chosen_rows.shape, bf16),
            pltpu.VMEM((pack + own_rows, HEAD), bf16),
            pltpu.VMEM((pack + own_rows, HEAD), bf16),
            pltpu.VMEM((1, pack + own_rows), f32),
            pltpu.VMEM((1, pack), f32),
            pltpu.VMEM((own_rows, feats), bf16),
            pltpu.VMEM((mp, own_rows, width), bf16),
            pltpu.VMEM((own_rows, width), bf16),
            pltpu.VMEM((own_rows, width), bf16),
            pltpu.VMEM((own_rows, width), bf16),
            pltpu.VMEM((8, 128), f32),
            pltpu.VMEM((mp, 8, 128), f32),
            pltpu.VMEM((8, 128), f32),
            pltpu.VMEM((ranks, 8, 128), f32),
            dma((6,)),
            dma((ranks - 1,)),
            dma((ranks - 1,)),
            dma((max(rows - 1, 1), mp)),
            dma((max(rows - 1, 1), mp)),
            dma((3, mp)),
            dma((3, mp)),
            dma((3, mp)),
            dma((3, mp)),
            dma((mp - 1,)),
            dma((mp - 1,)),
            dma((ranks - 1,)),
            dma((ranks - 1,)),
        ],
        compiler_params=pltpu.CompilerParams(
            collective_id=0, has_side_effects=True, vmem_limit_bytes=60 * 1024 * 1024
        ),
        name="block",
    )(
        hidden,
        old_logp.reshape(count, slot),
        rewards[None, :],
        resp_dest[None, :],
        resp_len[None, :],
        resp_offset[None, :],
        prompt_group[None, :],
        attn_gain[None, :],
        w_query,
        q_bias[None, :],
        w_key,
        k_bias[None, :],
        w_value,
        v_bias[None, :],
        w_out,
        freq,
        log_normalizer[None, :],
        chosen_rows,
        final_gain[None, :],
    )
    return (objective.reshape(-1), loss[0, 0])


def solution(mesh):
    return jax.shard_map(
        body,
        mesh=mesh,
        in_specs=(
            P(("row", "col"), "mp"),
            P(("row", "col")),
            P(("row", "col")),
            P(("row", "col")),
            P(("row", "col")),
            P(("row", "col")),
            P(("row", "col")),
            P(),
            P(None, "mp"),
            P("mp"),
            P(None, "mp"),
            P("mp"),
            P(None, "mp"),
            P("mp"),
            P("mp", None),
            P(),
            P(("row", "col", "mp"), None),
            P(("row", "col", "mp")),
        ),
        out_specs=(P(("row", "col", "mp")), P()),
        check_vma=False,
    )
```

time: 248 us -> 94 us (0.38)
  blocking collectives: 87.4 us -> 0 us
  Pallas kernels: 0 us -> 86.2 us
  waiting for transfers between devices: 57.4 us -> 0 us
  matrix products: 28.4 us -> 0 us
  local copies, waits for them, and re-layouts: 31.4 us -> 5.03 us
  other arithmetic: 19.6 us -> 0 us
  between operations: 16.9 us -> 2.39 us
  starting transfers between devices: 6.51 us -> 0 us
    pallas_call x0 -> x1, Pallas kernels: none -> 86.2 us  [body(): pl.pallas_call(functools.partial(main_kernel, rows, cols), out_shape=(jax...]
    psum x2 -> x0, blocking collectives: 60.2 us -> none  [the longest x1 39.6 us: body(): lax.psum((jnp.sum(objective), jnp.sum(own_occupied.astype(jnp.float32))),...]
    reduce_scatter x1 -> x0, waiting for transfers between devices: 32.1 us -> none  [body(): lax.psum_scatter(jnp.dot(pieces, w_out, preferred_element_type=jnp.float3...]
    dot_general x14 -> x0, matrix products: 28.4 us -> none  [the longest x1 8.28 us: body(): jnp.dot(pieces, w_out, preferred_element_type=jnp.float32)]
    all_to_all x1 -> x0, blocking collectives: 27.1 us -> none  [body(): lax.all_to_all(send_rows, 'row', split_axis=0, concat_axis=0, tiled=True)]
    all_gather x1 -> x0, waiting for transfers between devices: 20 us -> none  [body(): all_rows = lax.all_gather(flat_rows, 'mp', axis=1, tiled=True)]
    gather x2 -> x0, local copies, waits for them, and re-layouts: 13.1 us -> none  [the longest x1 12.1 us: body(): all_rows[token_index]]
    reduce_sum x8 -> x0, other arithmetic: 11.2 us -> none  [the longest x1 3.41 us: body(): jnp.mean(jnp.square(gathered.astype(jnp.float32)), -1, keepdims=True)]
  transfers between devices with their start and end apart: 4 -> 0, of which waited for: 4 -> 0; matrix products, arithmetic and copies ran while one was open for 3% -> 0% of each run, Pallas kernels for 0% -> 0%
where the time goes in v1:
time: 94 us; the launch traced here: 93.6 us
  Pallas kernels  86.2 us (92%)
  local copies, waits for them, and re-layouts  5.03 us (5%)
  between operations  2.39 us (3%)
    pallas_call x1, Pallas kernels, body(): pl.pallas_call(functools.partial(main_kernel, rows, cols), out_shape=(jax...  86.2 us

profile of v1, /device:TPU:0, one launch (start us, length us, event | category | flops | bytes accessed | tf_op | source)
XLA Modules:
  0.0 93.6 jit_solution(6764663589992561989)
XLA Ops:
  0.6 1.3 %broadcast_in_dim.39.qb = bf16[1,896]{1,0:T(2,128)(2,1)} reshape(bf16[896]{0:T(1024)(128)(2,1)} %param.28) | data formatting | bytes 3584 | tf_op jit(solution)/shard_map/broadcast_in_dim | solution.py:556
  1.9 1.3 %broadcast_in_dim.38.gain = bf16[1,3584]{1,0:T(2,128)(2,1)} reshape(bf16[3584]{0:T(1024)(128)(2,1)} %param.26) | data formatting | bytes 14336 | tf_op jit(solution)/shard_map/broadcast_in_dim | solution.py:554
  3.2 1.3 %broadcast_in_dim.43.fgain = bf16[1,3584]{1,0:T(2,128)(2,1)} reshape(bf16[3584]{0:T(1024)(128)(2,1)} %param.34) | data formatting | bytes 14336 | tf_op jit(solution)/shard_map/broadcast_in_dim | solution.py:565
  4.5 86.2 %block.1 = (f32[1,128]{1,0:T(1,128)}, f32[1,128]{1,0:T(1,128)}) custom-call(bf16[1024,896]{1,0:T(8,128)(2,1)} %hidden_hbm.1, f32[8,128]{1,0:T(8,128)} %bitcast.12, f32[1,8]{1,0:T(1,128)} %bitcast.13, s32[1,8]{1,0:T(1,128)} %bitcast.14, s32[1,8]{1,0:T(1,128)} %bitcast.15, s32[1,8]{1,0:T(1,128)} %bitcast.16, s32[1,8]{1,0:T(1,128)} %bitcast.17, ...), custom_call_target="tpu_custom_call" | custom-call | tf_op jit(solution)/shard_map/block/pallas_call | solution.py:493
  90.7 1.1 %copy.23 = f32[128]{0:T(128)} copy(f32[128]{0:T(128)} %bitcast.22) | data formatting | bytes 1024
